TPU v7x, 32 devices: a whole 2x2x4 slice. The times are simulated.
32 devices in a mesh: win: 2 (over y), vel: 8 (over z, x), sp: 2 (over core).
Axes of the slice: x: 2, y: 2, z: 4, core: 2. Of those that a mesh axis runs over, the one named last changes fastest.
Arguments:
- f_start: float32 [2, 1536, 64, 128], P('win', 'vel', 'sp'), may hold values from 0 to 15, as said below
- relax_rate: float32 [64, 128], P('sp'), may hold values from 0.1 to 10
Outputs:
- corrected: float32 [2, 4, 64, 128], P('win', None, 'sp')
- lifted: float32 [2, 1536, 64, 128], P('win', 'vel', 'sp')
Inputs may be any that keep to these rules, and one draw needn't show every extreme that they name: `f_start`: no entry is negative.
All inputs are finite; a program needn't handle non-finite values.
Results may differ from a plain program's by a relative error of at most 0.00021.
Values sent between devices are 32-bit elements; how exact they have to be, the bound alone decides.
A program may use at most 64 MiB of HBM per device.

v0:
```python
import math
import jax
import jax.numpy as jnp
from jax import lax
from jax.sharding import PartitionSpec as P

NVX = 48
NVY = 32
vel_max = 6.0
fine_ratio = 0.075
coarse_ratio = 0.15
density_floor = 0.3
thermal_lower_bound = 0.3


def with_halo(block, sides, width):
    for axis, dim in sides:
        count = lax.axis_size(axis)
        forward = [(i, i + 1) for i in range(count - 1)]
        forward.append((count - 1, 0))
        backward = [(target, source) for source, target in forward]
        low = lax.ppermute(
            lax.slice_in_dim(block, block.shape[dim] - width, None, axis=dim), axis, forward
        )
        high = lax.ppermute(lax.slice_in_dim(block, 0, width, axis=dim), axis, backward)
        block = jnp.concatenate([low, block, high], axis=dim)
    return block


def shifted(value, axis, steps):
    count = lax.axis_size(axis)
    leading, last = (max(0, -steps), min(count, count - steps))
    return lax.ppermute(value, axis, [(source, source + steps) for source in range(leading, last)])


def velocity_table(first, count):
    index = first + jnp.arange(count, dtype=jnp.int32)
    vel_x = -vel_max + ((index // NVY).astype(jnp.float32) + 0.5) * (2.0 * vel_max / NVX)
    vel_y = -vel_max + ((index % NVY).astype(jnp.float32) + 0.5) * (2.0 * vel_max / NVY)
    return (vel_x, vel_y)


def moment_table(vel_x, vel_y):
    weight_unit = 2.0 * vel_max / NVX * (2.0 * vel_max / NVY) / (2.0 * math.pi)
    return (
        jnp.stack([jnp.ones_like(vel_x), vel_x, vel_y, 0.5 * (vel_x * vel_x + vel_y * vel_y)])
        * weight_unit
    )


def moments(field, table):
    flat = field.reshape(field.shape[0], -1)
    out = jnp.dot(table, flat, precision=lax.Precision.HIGHEST, preferred_element_type=jnp.float32)
    return out.reshape(4, field.shape[1], field.shape[2])


def physical_variables(distribution_array):
    mass_per_volume = jnp.maximum(distribution_array[0], density_floor)
    horizontal_flow = distribution_array[1] / mass_per_volume
    upward_flow = distribution_array[2] / mass_per_volume
    inner_volumes = (
        distribution_array[3]
        - 0.5 * (distribution_array[1] * horizontal_flow + distribution_array[2] * upward_flow)
    ) / mass_per_volume
    pointwise_thermal_level = jnp.maximum(inner_volumes, thermal_lower_bound)
    return (mass_per_volume, horizontal_flow, upward_flow, pointwise_thermal_level)


def equilibrium_density(distribution_array, vel_x, vel_y):
    mass_per_volume, horizontal_flow, upward_flow, pointwise_thermal_level = physical_variables(
        distribution_array
    )
    horizontal_gradient = vel_x[:, None, None] - horizontal_flow[None]
    upward_gradient = vel_y[:, None, None] - upward_flow[None]
    return (mass_per_volume / pointwise_thermal_level)[None] * jnp.exp(
        -(horizontal_gradient * horizontal_gradient + upward_gradient * upward_gradient)
        / (2.0 * pointwise_thermal_level[None])
    )


def transport(field, left, right, vel_x, vel_y):
    coef_x = (vel_x * fine_ratio)[:, None, None]
    coef_y = (vel_y * fine_ratio)[:, None, None]
    below = jnp.roll(field, 1, axis=2)
    above = jnp.roll(field, -1, axis=2)
    out = (
        field
        - jnp.maximum(coef_x, 0.0) * (field - left)
        - jnp.minimum(coef_x, 0.0) * (right - field)
    )
    return (
        out
        - jnp.maximum(coef_y, 0.0) * (field - below)
        - jnp.minimum(coef_y, 0.0) * (above - field)
    )


def euler_update(padded_array):
    mass_per_volume, horizontal_flow, upward_flow, pointwise_thermal_level = physical_variables(
        padded_array
    )
    normal_stress = mass_per_volume * pointwise_thermal_level
    acoustic_wave_rate = jnp.sqrt(2.0 * pointwise_thermal_level)
    flux_x = jnp.stack(
        [
            padded_array[1],
            padded_array[1] * horizontal_flow + normal_stress,
            padded_array[2] * horizontal_flow,
            (padded_array[3] + normal_stress) * horizontal_flow,
        ]
    )
    flux_y = jnp.stack(
        [
            padded_array[2],
            padded_array[1] * upward_flow,
            padded_array[2] * upward_flow + normal_stress,
            (padded_array[3] + normal_stress) * upward_flow,
        ]
    )
    reach_x = jnp.abs(horizontal_flow) + acoustic_wave_rate
    reach_y = jnp.abs(upward_flow) + acoustic_wave_rate
    face_x = 0.5 * (flux_x[:, :-1, 1:-1] + flux_x[:, 1:, 1:-1]) - 0.5 * jnp.maximum(
        reach_x[:-1, 1:-1], reach_x[1:, 1:-1]
    )[None] * (padded_array[:, 1:, 1:-1] - padded_array[:, :-1, 1:-1])
    face_y = 0.5 * (flux_y[:, 1:-1, :-1] + flux_y[:, 1:-1, 1:]) - 0.5 * jnp.maximum(
        reach_y[1:-1, :-1], reach_y[1:-1, 1:]
    )[None] * (padded_array[:, 1:-1, 1:] - padded_array[:, 1:-1, :-1])
    return padded_array[:, 1:-1, 1:-1] - coarse_ratio * (
        face_x[:, 1:] - face_x[:, :-1] + (face_y[:, :, 1:] - face_y[:, :, :-1])
    )


def coarse_step(distribution_array):
    padded_array = with_halo(distribution_array, (("sp", 1),), 1)
    padded_array = jnp.concatenate(
        [padded_array[:, :, -1:], padded_array, padded_array[:, :, :1]], axis=2
    )
    return euler_update(padded_array)


def advance(current, vel_x, vel_y):
    padded_array = with_halo(current, (("sp", 1),), 1)
    return transport(current, padded_array[:, :-2], padded_array[:, 2:], vel_x, vel_y)


def per_device(f_start, relax_rate):
    field = f_start[0]
    count = field.shape[0]
    vel_x, vel_y = velocity_table(lax.axis_index("vel") * count, count)
    table = moment_table(vel_x, vel_y)
    rates = relax_rate[None]
    local_start = moments(field, table)
    start = lax.psum(local_start, "vel")
    current = field
    for step in range(2):
        star = advance(current, vel_x, vel_y)
        distribution_array = lax.psum(moments(star, table), "vel")
        current = (star + rates * equilibrium_density(distribution_array, vel_x, vel_y)) / (
            1.0 + rates
        )
    delta = distribution_array - coarse_step(start)
    windows = lax.axis_size("win")
    position = lax.axis_index("win")
    carried = start
    for turn in range(windows):
        result = coarse_step(carried) + delta
        if turn + 1 < windows:
            passed = shifted(result, "win", 1)
            carried = jnp.where(position == 0, start, passed)
    lifted = (
        current
        + equilibrium_density(result, vel_x, vel_y)
        - equilibrium_density(distribution_array, vel_x, vel_y)
    )
    return (result[None], lifted[None])


def solution(mesh):
    return jax.shard_map(
        per_device,
        mesh=mesh,
        in_specs=(P("win", "vel", "sp", None), P("sp", None)),
        out_specs=(P("win", None, "sp", None), P("win", "vel", "sp", None)),
        check_vma=False,
    )
```

profile of v0, /device:TPU:0, one launch (start us, length us, event | category | flops | bytes accessed | tf_op | source)
XLA Modules:
  0.0 217.6 jit_solution(6024811357756668443)
XLA Ops:
  7.2 2.2 fusion.107
  9.9 6.6 %fusion.105 = (f32[192,32,127]{2,1,0:T(8,128)}, f32[192,32,127]{2,1,0:T(8,128)}) fusion(f32[192,32,128]{2,1,0:T(8,128)} %bitcast.194), kind=kLoop, calls=%fused_computation.217 | loop fusion | bytes 12484608 | tf_op jit(solution)/shard_map/jit(_roll_static)/slice | solution.py:85
  16.5 3.9 %fusion.106 = (f32[192,32,1]{2,1,0:T(8,128)}, f32[192,32,1]{2,1,0:T(8,128)}) fusion(f32[192,32,128]{2,1,0:T(8,128)S(1)} %bitcast.195), kind=kLoop, calls=%fused_computation.218 | loop fusion | bytes 98304 | tf_op jit(solution)/shard_map/jit(_roll_static)/slice | solution.py:85
  20.4 3.9 %fusion.6 = f32[4,32,128]{2,0,1:T(4,128)} fusion(f32[1,192]{1,0:T(1,128)S(1)} %get-tuple-element.77, f32[1,192]{1,0:T(1,128)S(1)} %get-tuple-element.76, f32[1,192]{1,0:T(1,128)S(1)} %multiply_add_fusion.4, f32[4]{0:T(128)S(1)} %pad.72.clone, f32[24,8,32,128]{3,2,1,0:T(8,128)S(1)} %bitcast.196), kind=kOutput, calls=%fused_computation.9 | convolution fusion | flops 37751808 | bytes 3213584 | tf_op jit(solution)/shard_map/dot_general | solution.py:53
  24.4 6.2 %fusion.21 = f32[192,32,128]{2,1,0:T(8,128)S(1)} fusion(f32[192,32,128]{2,1,0:T(8,128)S(1)} %bitcast.197, f32[192,1,128]{2,1,0:T(1,128)S(1)} %collective-permute-done.3, f32[192,1,128]{2,1,0:T(1,128)S(1)} %collective-permute-done.2, f32[192,32,127]{2,1,0:T(8,128)} %get-tuple-element.42, f32[192,32,1]{2,1,0:T(8,128)} %get-tuple-element.44, ...), kind=kLoop, calls=%fused_computation.27 | loop fusion | flops 12582912 | bytes 12782592 | tf_op jit(solution)/shard_map/sub | solution.py:92
  30.7 1.7 copy-done.1
  32.3 3.9 %fusion.3 = f32[4,32,128]{2,0,1:T(4,128)} fusion(f32[1,192]{1,0:T(1,128)S(1)} %get-tuple-element.77, f32[1,192]{1,0:T(1,128)S(1)} %get-tuple-element.76, f32[1,192]{1,0:T(1,128)S(1)} %multiply_add_fusion.4, f32[4]{0:T(128)S(1)} %pad.72.clone, f32[24,8,32,128]{3,2,1,0:T(8,128)S(1)} %bitcast.199), kind=kOutput, calls=%fused_computation.6 | convolution fusion | flops 37751808 | bytes 3213584 | tf_op jit(solution)/shard_map/dot_general | solution.py:53
  36.5 71.9 %all-reduce.4.cloned.1.call-done = f32[4,32,128]{2,0,1:T(4,128)} async-done(((f32[4,32,128]{2,0,1:T(4,128)}), f32[4,32,128]{2,0,1:T(4,128)}) %all-reduce.4.cloned.1.call-update) | async-done | bytes 65552 | tf_op jit(solution)/shard_map/psum | solution.py:157
  108.4 1.1 fusion.90
  109.5 2.9 %add_divide_fusion = f32[192,32,128]{2,1,0:T(8,128)S(1)} fusion(f32[192,32,128]{2,1,0:T(8,128)} %copy-done.1, f32[32,128]{1,0:T(8,128)S(1)} %broadcast_add_fusion, f32[32,128]{1,0:T(8,128)S(1)} %bitcast.210, f32[32,128]{1,0:T(8,128)S(1)} %bitcast.219, f32[192]{0:T(256)S(1)} %get-tuple-element.78, f32[32,128]{1,0:T(8,128)S(1)} %bitcast.218, ...), kind=kLoop, calls=%fused_computation.41 | loop fusion | flops 8650752 | bytes 6391296 | tf_op jit(solution)/shard_map/div | solution.py:158
  112.4 1.1 fusion.102
  113.7 0.5 collective-permute-start.5
  114.2 1.1 fusion.103
  115.4 3.9 %fusion.13 = f32[192,32,128]{2,1,0:T(8,128)S(1)} fusion(f32[192,32,128]{2,1,0:T(8,128)S(1)} %add_divide_fusion, f32[192,1,128]{2,1,0:T(1,128)S(1)} %collective-permute-done.5, f32[192,1,128]{2,1,0:T(1,128)S(1)} %collective-permute-done.4, f32[192,32,127]{2,1,0:T(8,128)S(1)} %get-tuple-element.36, f32[192,32,1]{2,1,0:T(8,128)S(1)} %get-tuple-element.38, ...), kind=kLoop, calls=%fused_computation.17 | loop fusion | flops 12582912 | bytes 12782592 | tf_op jit(solution)/shard_map/sub | solution.py:92
  119.3 3.9 %fusion = f32[4,32,128]{2,0,1:T(4,128)} fusion(f32[1,192]{1,0:T(1,128)S(1)} %get-tuple-element.77, f32[1,192]{1,0:T(1,128)S(1)} %get-tuple-element.76, f32[1,192]{1,0:T(1,128)S(1)} %multiply_add_fusion.4, f32[4]{0:T(128)S(1)} %pad.72.clone, f32[24,8,32,128]{3,2,1,0:T(8,128)S(1)} %bitcast.198), kind=kOutput, calls=%fused_computation.3 | convolution fusion | flops 37751808 | bytes 3213584 | tf_op jit(solution)/shard_map/dot_general | solution.py:53
  123.2 70.8 %all-reduce.6.cloned.1.call-done = (f32[4,32,128]{2,0,1:T(4,128)}, f32[4,32,128]{2,0,1:T(4,128)}) async-done(((f32[4,32,128]{2,0,1:T(4,128)}, f32[4,32,128]{2,0,1:T(4,128)}), (f32[4,32,128]{2,0,1:T(4,128)}, f32[4,32,128]{2,0,1:T(4,128)})) %all-reduce.6.cloned.1.call-update) | async-done | bytes 131088 | tf_op jit(solution)/shard_map/psum | solution.py:157
  194.0 0.7 fusion.113
  194.8 0.5 collective-permute-start.1
  195.3 0.8 copy.29
  197.5 3.4 %collective-permute-start.6 = (f32[4,32,128]{2,0,1:T(4,128)S(1)}, f32[4,32,128]{2,0,1:T(4,128)S(1)}, u32[]{:S(2)}, u32[]{:S(2)}) collective-permute-start(f32[4,32,128]{2,0,1:T(4,128)S(1)} %get-tuple-element.23), channel_id=1, source_target_pairs={{0,16},{1,17},{2,18},{3,19},{4,20},{5,21},{6,22},{7,23},{8,24},{9,... | collective-permute-start | bytes 196616 | tf_op jit(solution)/shard_map/ppermute | solution.py:33
  200.9 1.8 collective-permute-done.6
  203.4 0.6 collective-permute-done.7
  206.2 0.6 copy.52
  206.9 3.8 %subtract_bitcast_fusion = f32[1,192,32,128]{3,2,1,0:T(8,128)} fusion(f32[192,32,128]{2,1,0:T(8,128)S(1)} %fusion.13, f32[32,128]{1,0:T(8,128)S(1)} %bitcast.209, f32[32,128]{1,0:T(8,128)S(1)} %bitcast.216, f32[32,128]{1,0:T(8,128)S(1)} %bitcast.215, f32[32,128]{1,0:T(8,128)S(1)} %bitcast.214, f32[32,128]{1,0:T(8,128)S(1)} %bitcast.208, ...), kind=kLoop, calls=%fused_computation.40 | loop fusion | flops 16515072 | bytes 6456832 | tf_op jit(solution)/shard_map/broadcast_in_dim | solution.py:175
  (78 shorter events, 5.2 us)
Async XLA Ops:
  7.2 101.2 %all-reduce.4.cloned.1.call-start = ((), (), s32[]{:S(2)}) async-start(), calls=%async_computation | async-start | bytes 131072 | tf_op jit(solution)/shard_map/psum | solution.py:157
  9.4 15.0 %collective-permute-start.2 = (f32[192,1,128]{2,1,0:T(1,128)}, f32[192,1,128]{2,1,0:T(1,128)S(1)}, u32[]{:S(2)}, u32[]{:S(2)}) collective-permute-start(f32[192,1,128]{2,1,0:T(1,128)} %get-tuple-element.45), channel_id=1, source_target_pairs={{0,1},{1,0},{2,3},{3,2},{4,5},{5,4},{6,7},{7,6},{8,9},{9,8},{10,11... | collective-permute-start | bytes 294920 | tf_op jit(solution)/shard_map/ppermute | solution.py:22
  9.9 14.5 %collective-permute-start.3 = (f32[192,1,128]{2,1,0:T(1,128)S(1)}, f32[192,1,128]{2,1,0:T(1,128)S(1)}, u32[]{:S(2)}, u32[]{:S(2)}) collective-permute-start(f32[192,1,128]{2,1,0:T(1,128)S(1)} %get-tuple-element.46), channel_id=1, source_target_pairs={{1,0},{0,1},{3,2},{2,3},{5,4},{4,5},{7,6},{6,7},{9,8},{8,9},{11,10... | collective-permute-start | bytes 294920 | tf_op jit(solution)/shard_map/ppermute | solution.py:25
  9.9 6.6 %copy-start = (f32[1,192,32,128]{3,2,1,0:T(8,128)S(1)}, f32[1,192,32,128]{3,2,1,0:T(8,128)}, u32[]{:S(2)}) copy-start(f32[1,192,32,128]{3,2,1,0:T(8,128)} %param.2) | copy-start | bytes 9437188
  16.5 3.9 %copy-start.5 = (f32[32,128]{1,0:T(8,128)S(1)}, f32[32,128]{1,0:T(8,128)}, u32[]{:S(2)}) copy-start(f32[32,128]{1,0:T(8,128)} %param.3) | copy-start | bytes 49156
  20.3 4.1 %copy-start.2 = (f32[192,32,127]{2,1,0:T(8,128)S(1)}, f32[192,32,127]{2,1,0:T(8,128)}, u32[]{:S(2)}) copy-start(f32[192,32,127]{2,1,0:T(8,128)} %get-tuple-element.41) | copy-start | bytes 9363460
  30.6 1.7 copy-start.1
  36.3 157.8 %all-reduce.6.cloned.1.call-start = ((), (), s32[]{:S(2)}) async-start(), calls=%async_computation.1 | async-start | bytes 262144 | tf_op jit(solution)/shard_map/psum | solution.py:157
  113.7 1.7 collective-permute-start.4
  113.7 1.6 collective-permute-start.5
  194.0 3.3 %copy-start.3 = (f32[4,32,128]{2,0,1:T(4,128)S(1)}, f32[4,32,128]{2,0,1:T(4,128)}, u32[]{:S(2)}) copy-start(f32[4,32,128]{2,0,1:T(4,128)} %get-tuple-element.7) | copy-start | bytes 196612
  194.0 3.3 %copy-start.4 = (f32[4,32,128]{2,0,1:T(4,128)S(1)}, f32[4,32,128]{2,0,1:T(4,128)}, u32[]{:S(2)}) copy-start(f32[4,32,128]{2,0,1:T(4,128)} %get-tuple-element.6) | copy-start | bytes 196612
  194.8 1.4 collective-permute-start
  194.8 1.4 collective-permute-start.1
  197.5 5.3 %collective-permute-start.6 = (f32[4,32,128]{2,0,1:T(4,128)S(1)}, f32[4,32,128]{2,0,1:T(4,128)S(1)}, u32[]{:S(2)}, u32[]{:S(2)}) collective-permute-start(f32[4,32,128]{2,0,1:T(4,128)S(1)} %get-tuple-element.23), channel_id=1, source_target_pairs={{0,16},{1,17},{2,18},{3,19},{4,20},{5,21},{6,22},{7,23},{8,24},{9,... | collective-permute-start | bytes 196616 | tf_op jit(solution)/shard_map/ppermute | solution.py:33
  202.8 1.2 collective-permute-start.7
  202.8 1.3 collective-permute-start.8
Sparse Core Ops, SparseCore 0:
  36.4 71.9 all-reduce.3
  123.3 70.6 all-reduce.5
where the time goes:
time: 218 us
  waiting for transfers between devices  145 us (67%)
  other arithmetic  21.1 us (10%)
  local copies, waits for them, and re-layouts  19.1 us (9%)
  between operations  14.5 us (7%)
  matrix products  11.8 us (5%)
  starting transfers between devices  5.8 us (3%)
    psum x2, waiting for transfers between devices, per_device(): distribution_array = lax.psum(moments(star, table), 'vel')  143 us
    slice x4, local copies, waits for them, and re-layouts, transport(): above = jnp.roll(field, -1, axis=2)  12.6 us
    dot_general x3, matrix products, moments(): jnp.dot(table, flat, precision=lax.Precision.HIGHEST, preferred_element_t...  11.8 us
    sub x2, other arithmetic, transport(): out - jnp.maximum(coef_y, 0.0) * (field - below)  10.1 us
  transfers between devices with their start and end apart: 11, of which 5 were waited for; matrix products, arithmetic and copies ran while one was open for 8% of the time, Pallas kernels for 0%

commit v1 on v0

--- a/solution.py
+++ b/solution.py
@@ -1,3 +1,4 @@
+import functools
 import math
 import jax
 import jax.numpy as jnp
@@ -11,6 +12,14 @@
 coarse_ratio = 0.15
 density_floor = 0.3
 thermal_lower_bound = 0.3
+
+
+def regions_load(arr, mesh_dim):
+    earlier = lax.all_gather(arr, axis_name=mesh_dim)
+    return jnp.sum(earlier, 0)
+
+
+review_the_bands = functools.partial(regions_load, mesh_dim="vel")
 
 
 def with_halo(block, sides, width):
@@ -154,7 +163,7 @@
     current = field
     for step in range(2):
         star = advance(current, vel_x, vel_y)
-        distribution_array = lax.psum(moments(star, table), "vel")
+        distribution_array = review_the_bands(moments(star, table))
         current = (star + rates * equilibrium_density(distribution_array, vel_x, vel_y)) / (
             1.0 + rates
         )

time: 218 us -> 204 us (0.936)
  waiting for transfers between devices: 145 us -> 67.5 us
  blocking collectives: 0 us -> 65 us
  local copies, waits for them, and re-layouts: 19.1 us -> 16.5 us
    psum x2 -> x1, waiting for transfers between devices: 143 us -> 64.5 us  [per_device(): start = lax.psum(local_start, 'vel')]
    all_gather x0 -> x2, blocking collectives: none -> 65 us  [regions_load(): earlier = lax.all_gather(arr, axis_name=mesh_dim)]
    slice x4, local copies, waits for them, and re-layouts: 12.6 us -> 9.78 us  [transport(): above = jnp.roll(field, -1, axis=2)]
  transfers between devices with their start and end apart: 11 -> 10, of which waited for: 5 -> 4; matrix products, arithmetic and copies ran while one was open for 8% -> 8% of each run, Pallas kernels for 0% -> 0%
where the time goes in v1:
time: 204 us
  waiting for transfers between devices  67.5 us (33%)
  blocking collectives  65 us (32%)
  other arithmetic  22.6 us (11%)
  local copies, waits for them, and re-layouts  16.5 us (8%)
  between operations  14.5 us (7%)
  matrix products  12.3 us (6%)
  starting transfers between devices  5.57 us (3%)
    all_gather x2, blocking collectives, regions_load(): earlier = lax.all_gather(arr, axis_name=mesh_dim)  65 us
    psum x1, waiting for transfers between devices, per_device(): start = lax.psum(local_start, 'vel')  64.5 us
    dot_general x3, matrix products, moments(): jnp.dot(table, flat, precision=lax.Precision.HIGHEST, preferred_element_t...  12.3 us
    sub x2, other arithmetic, transport(): out - jnp.maximum(coef_y, 0.0) * (field - below)  10.2 us
    slice x4, local copies, waits for them, and re-layouts, transport(): above = jnp.roll(field, -1, axis=2)  9.78 us
    broadcast_in_dim x1, other arithmetic, per_device(): return (result[None], lifted[None])  4.56 us
  transfers between devices with their start and end apart: 10, of which 4 were waited for; matrix products, arithmetic and copies ran while one was open for 8% of the time, Pallas kernels for 0%

profile of v1, /device:TPU:0, one launch (start us, length us, event | category | flops | bytes accessed | tf_op | source)
XLA Modules:
  0.0 204.1 jit_solution(4428475189332983849)
XLA Ops:
  7.2 2.3 %fusion.110 = (f32[192,1,128]{2,1,0:T(1,128)}, f32[192,1,128]{2,1,0:T(1,128)}) fusion(f32[192,32,128]{2,1,0:T(8,128)} %bitcast.201), kind=kLoop, calls=%fused_computation.218 | loop fusion | bytes 393216 | tf_op jit(solution)/shard_map/slice | solution.py:32
  10.1 5.7 %fusion.6 = f32[4,32,128]{2,0,1:T(4,128)} fusion(f32[1,192]{1,0:T(1,128)S(1)} %get-tuple-element.87, f32[1,192]{1,0:T(1,128)S(1)} %get-tuple-element.86, f32[1,192]{1,0:T(1,128)S(1)} %multiply_add_fusion.4, f32[4]{0:T(128)S(1)} %pad.72.clone, f32[24,8,32,128]{3,2,1,0:T(8,128)} %bitcast.202), kind=kOutput, calls=%fused_computation.9 | convolution fusion | flops 37751808 | bytes 3213584 | tf_op jit(solution)/shard_map/dot_general | solution.py:62
  15.9 3.8 %fusion.108 = (f32[192,32,127]{2,1,0:T(8,128)}, f32[192,32,127]{2,1,0:T(8,128)}) fusion(f32[192,32,128]{2,1,0:T(8,128)S(1)} %bitcast.203), kind=kLoop, calls=%fused_computation.216 | loop fusion | bytes 12484608 | tf_op jit(solution)/shard_map/jit(_roll_static)/slice | solution.py:94
  19.7 3.8 %fusion.109 = (f32[192,32,1]{2,1,0:T(8,128)}, f32[192,32,1]{2,1,0:T(8,128)}) fusion(f32[192,32,128]{2,1,0:T(8,128)S(1)} %bitcast.204), kind=kLoop, calls=%fused_computation.217 | loop fusion | bytes 98304 | tf_op jit(solution)/shard_map/jit(_roll_static)/slice | solution.py:94
  23.5 64.5 %all-reduce.2.cloned.1.call-done = f32[4,32,128]{2,0,1:T(4,128)} async-done(((f32[4,32,128]{2,0,1:T(4,128)}), f32[4,32,128]{2,0,1:T(4,128)}) %all-reduce.2.cloned.1.call-update) | async-done | bytes 65552 | tf_op jit(solution)/shard_map/psum | solution.py:162
  88.0 0.8 fusion.118
  89.4 0.8 copy.83
  91.4 6.3 %fusion.21 = f32[192,32,128]{2,1,0:T(8,128)S(1)} fusion(f32[192,32,128]{2,1,0:T(8,128)S(1)} %bitcast.205, f32[192,1,128]{2,1,0:T(1,128)} %collective-permute-done.3, f32[192,1,128]{2,1,0:T(1,128)} %collective-permute-done.2, f32[192,32,127]{2,1,0:T(8,128)} %get-tuple-element.44, f32[192,32,1]{2,1,0:T(8,128)} %get-tuple-element.46, ...), kind=kLoop, calls=%fused_computation.27 | loop fusion | flops 12582912 | bytes 12782592 | tf_op jit(solution)/shard_map/sub | solution.py:101
  97.7 1.7 copy-done.1
  99.4 3.3 %fusion.3 = f32[4,32,128]{2,0,1:T(4,128)S(1)} fusion(f32[1,192]{1,0:T(1,128)S(1)} %get-tuple-element.87, f32[1,192]{1,0:T(1,128)S(1)} %get-tuple-element.86, f32[1,192]{1,0:T(1,128)S(1)} %multiply_add_fusion.4, f32[4]{0:T(128)S(1)} %pad.72.clone, f32[24,8,32,128]{3,2,1,0:T(8,128)S(1)} %bitcast.207), kind=kOutput, calls=%fused_computation.6 | convolution fusion | flops 37751808 | bytes 3213584 | tf_op jit(solution)/shard_map/dot_general | solution.py:62
  102.7 31.7 %all-gather = f32[32,32,128]{2,1,0:T(8,128)S(1)} all-gather(f32[4,32,128]{2,1,0:T(8,128)S(1)} %copy.91), channel_id=2, replica_groups=mesh['win'=2,'vel'=8,'sp'=2] {'vel'}, dimensions={0}, use_global_device_ids=true | all-gather | bytes 589824 | tf_op jit(solution)/shard_map/all_gather | solution.py:18
  134.6 2.9 %add_divide_fusion = f32[192,32,128]{2,1,0:T(8,128)S(1)} fusion(f32[192,32,128]{2,1,0:T(8,128)} %copy-done.1, f32[32,128]{1,0:T(8,128)S(1)} %broadcast_add_fusion, f32[32,128]{1,0:T(8,128)S(1)} %bitcast.220, f32[32,128]{1,0:T(8,128)S(1)} %bitcast.229, f32[192]{0:T(256)S(1)} %get-tuple-element.88, f32[32,128]{1,0:T(8,128)S(1)} %bitcast.228, ...), kind=kLoop, calls=%fused_computation.41 | loop fusion | flops 8650752 | bytes 6391296 | tf_op jit(solution)/shard_map/div | solution.py:167
  137.5 1.1 fusion.105
  139.4 1.1 fusion.106
  140.5 3.9 %fusion.13 = f32[192,32,128]{2,1,0:T(8,128)S(1)} fusion(f32[192,32,128]{2,1,0:T(8,128)S(1)} %add_divide_fusion, f32[192,1,128]{2,1,0:T(1,128)S(1)} %collective-permute-done.5, f32[192,1,128]{2,1,0:T(1,128)S(1)} %collective-permute-done.4, f32[192,32,127]{2,1,0:T(8,128)S(1)} %get-tuple-element.38, f32[192,32,1]{2,1,0:T(8,128)S(1)} %get-tuple-element.40, ...), kind=kLoop, calls=%fused_computation.17 | loop fusion | flops 12582912 | bytes 12782592 | tf_op jit(solution)/shard_map/sub | solution.py:101
  144.4 3.3 %fusion = f32[4,32,128]{2,0,1:T(4,128)S(1)} fusion(f32[1,192]{1,0:T(1,128)S(1)} %get-tuple-element.87, f32[1,192]{1,0:T(1,128)S(1)} %get-tuple-element.86, f32[1,192]{1,0:T(1,128)S(1)} %multiply_add_fusion.4, f32[4]{0:T(128)S(1)} %pad.72.clone, f32[24,8,32,128]{3,2,1,0:T(8,128)S(1)} %bitcast.206), kind=kOutput, calls=%fused_computation.3 | convolution fusion | flops 37751808 | bytes 3213584 | tf_op jit(solution)/shard_map/dot_general | solution.py:62
  147.7 33.3 %all-gather.1 = f32[32,32,128]{2,1,0:T(8,128)} all-gather(f32[4,32,128]{2,1,0:T(8,128)S(1)} %copy.97), channel_id=3, replica_groups=mesh['win'=2,'vel'=8,'sp'=2] {'vel'}, dimensions={0}, use_global_device_ids=true | all-gather | bytes 589824 | tf_op jit(solution)/shard_map/all_gather | solution.py:18
  181.0 1.1 reduce_sum.19
  182.1 0.8 fusion.91
  182.8 3.4 %collective-permute-start.6 = (f32[4,32,128]{2,0,1:T(4,128)}, f32[4,32,128]{2,0,1:T(4,128)S(1)}, u32[]{:S(2)}, u32[]{:S(2)}) collective-permute-start(f32[4,32,128]{2,0,1:T(4,128)} %get-tuple-element.25), channel_id=1, source_target_pairs={{0,16},{1,17},{2,18},{3,19},{4,20},{5,21},{6,22},{7,23},{8,24},{9,... | collective-permute-start | bytes 196616 | tf_op jit(solution)/shard_map/ppermute | solution.py:42
  186.2 2.2 %collective-permute-done.6 = f32[4,32,128]{2,0,1:T(4,128)S(1)} collective-permute-done((f32[4,32,128]{2,0,1:T(4,128)}, f32[4,32,128]{2,0,1:T(4,128)S(1)}, u32[]{:S(2)}, u32[]{:S(2)}) %collective-permute-start.6) | collective-permute-done | bytes 65568 | tf_op jit(solution)/shard_map/ppermute | solution.py:42
  189.0 0.6 collective-permute-done.7
  192.0 0.6 copy.117
  192.7 4.6 %subtract_bitcast_fusion = f32[1,192,32,128]{3,2,1,0:T(8,128)} fusion(f32[192,32,128]{2,1,0:T(8,128)S(1)} %fusion.13, f32[32,128]{1,0:T(8,128)S(1)} %bitcast.219, f32[32,128]{1,0:T(8,128)S(1)} %bitcast.226, f32[32,128]{1,0:T(8,128)S(1)} %bitcast.225, f32[32,128]{1,0:T(8,128)S(1)} %bitcast.224, f32[32,128]{1,0:T(8,128)S(1)} %bitcast.218, ...), kind=kLoop, calls=%fused_computation.40 | loop fusion | flops 16515072 | bytes 6456832 | tf_op jit(solution)/shard_map/broadcast_in_dim | solution.py:184
  (83 shorter events, 6.0 us)
Async XLA Ops:
  7.2 8.7 %copy-start = (f32[1,192,32,128]{3,2,1,0:T(8,128)S(1)}, f32[1,192,32,128]{3,2,1,0:T(8,128)}, u32[]{:S(2)}) copy-start(f32[1,192,32,128]{3,2,1,0:T(8,128)} %param.2) | copy-start | bytes 9437188
  7.2 80.8 %all-reduce.2.cloned.1.call-start = ((), (), s32[]{:S(2)}) async-start(), calls=%async_computation | async-start | bytes 131072 | tf_op jit(solution)/shard_map/psum | solution.py:162
  9.6 81.8 %collective-permute-start.2 = (f32[192,1,128]{2,1,0:T(1,128)}, f32[192,1,128]{2,1,0:T(1,128)}, u32[]{:S(2)}, u32[]{:S(2)}) collective-permute-start(f32[192,1,128]{2,1,0:T(1,128)} %get-tuple-element.47), channel_id=1, source_target_pairs={{0,1},{1,0},{2,3},{3,2},{4,5},{5,4},{6,7},{7,6},{8,9},{9,8},{10,11... | collective-permute-start | bytes 294920 | tf_op jit(solution)/shard_map/ppermute | solution.py:31
  10.1 81.4 %collective-permute-start.3 = (f32[192,1,128]{2,1,0:T(1,128)}, f32[192,1,128]{2,1,0:T(1,128)}, u32[]{:S(2)}, u32[]{:S(2)}) collective-permute-start(f32[192,1,128]{2,1,0:T(1,128)} %get-tuple-element.48), channel_id=1, source_target_pairs={{1,0},{0,1},{3,2},{2,3},{5,4},{4,5},{7,6},{6,7},{9,8},{8,9},{11,10... | collective-permute-start | bytes 294920 | tf_op jit(solution)/shard_map/ppermute | solution.py:34
  19.7 3.8 %copy-start.4 = (f32[32,128]{1,0:T(8,128)S(1)}, f32[32,128]{1,0:T(8,128)}, u32[]{:S(2)}) copy-start(f32[32,128]{1,0:T(8,128)} %param.3) | copy-start | bytes 49156
  23.5 111.1 %copy-start.5 = (f32[32,128]{1,0:T(8,128)}, f32[32,128]{1,0:T(8,128)S(1)}, u32[]{:S(2)}) copy-start(f32[32,128]{1,0:T(8,128)S(1)} %broadcast_add_fusion) | copy-start | bytes 49156
  88.0 3.4 %copy-start.3 = (f32[4,32,128]{2,0,1:T(4,128)S(1)}, f32[4,32,128]{2,0,1:T(4,128)}, u32[]{:S(2)}) copy-start(f32[4,32,128]{2,0,1:T(4,128)} %all-reduce.2.cloned.1.call-done) | copy-start | bytes 196612
  88.0 3.4 %copy-start.2 = (f32[192,32,127]{2,1,0:T(8,128)S(1)}, f32[192,32,127]{2,1,0:T(8,128)}, u32[]{:S(2)}) copy-start(f32[192,32,127]{2,1,0:T(8,128)} %get-tuple-element.43) | copy-start | bytes 9363460
  88.8 1.4 collective-permute-start
  88.8 1.4 collective-permute-start.1
  97.7 1.7 copy-start.1
  138.8 1.7 collective-permute-start.4
  138.9 1.6 collective-permute-start.5
  182.8 5.6 %collective-permute-start.6 = (f32[4,32,128]{2,0,1:T(4,128)}, f32[4,32,128]{2,0,1:T(4,128)S(1)}, u32[]{:S(2)}, u32[]{:S(2)}) collective-permute-start(f32[4,32,128]{2,0,1:T(4,128)} %get-tuple-element.25), channel_id=1, source_target_pairs={{0,16},{1,17},{2,18},{3,19},{4,20},{5,21},{6,22},{7,23},{8,24},{9,... | collective-permute-start | bytes 196616 | tf_op jit(solution)/shard_map/ppermute | solution.py:42
  188.4 1.2 collective-permute-start.7
  188.5 1.3 collective-permute-start.8
Sparse Core Ops, SparseCore 0:
  16.0 71.9 all-reduce.1
